TPU v7x, 512 devices: a whole 4x8x8 slice. The times are simulated.
512 devices in a mesh: req: 128 (over z, y, core), tp: 4 (over x).
Axes of the slice: x: 4, y: 8, z: 8, core: 2. Of those that a mesh axis runs over, the one named last changes fastest.
Arguments:
- queries: bfloat16 [49152, 2048], P('req', 'tp'), may hold values from -32 to 32
- tree_kv: bfloat16 [49152, 256], P('req'), may hold values from -6 to 6
- suffix_kv: bfloat16 [768, 256, 256], P('req'), may hold values from -6 to 6
- suffix_len: int32 [768], P('req'), may hold values from 1 to 256
- group_ids: int32 [768], P('req'), may hold values from 0 to 1
- parents: int32 [768, 64], P('req'), may hold values from 0 to 62, as said below
- accepted: int32 [768, 8], P('req'), may hold values from 0 to 63, as said below
- prompt_kv: bfloat16 [2, 4096, 256], P(None, 'req'), may hold values from -12 to 12
- out_weight: bfloat16 [2048, 2048], P('tp'), may hold values from -0.5 to 0.5
Outputs:
- layer_output: bfloat16 [49152, 2048], P(('req', 'tp'))
- path_cache: bfloat16 [768, 8, 256], P('req')
Inputs may be any that keep to these rules, and one draw needn't show every extreme that they name: parents[r, 0] = 0 and parents[r, i] < i for i >= 1, so node 0 is every tree's root. accepted[r] runs from the root down one branch: accepted[r, 0] = 0 and accepted[r, t - 1] = parents[r, accepted[r, t]].
All inputs are finite; a program needn't handle non-finite values.
Results may differ from a plain program's by a relative error of at most 0.017.
Values may be sent and summed in bfloat16 or wider, within the bound.
A program may use at most 64 MiB of HBM per device.

v0:
```python
import jax
import jax.numpy as jnp
from jax import lax
from jax.sharding import PartitionSpec as P

neg_large = -1e30
block_len = 512


def ancestry(parents):
    node_count = parents.shape[1]
    positions = jnp.arange(node_count, dtype=jnp.int32)
    step_up = (parents[:, :, None] == positions[None, None, :]) & (positions[None, :, None] > 0)
    closure = (
        jnp.where(step_up, 1.0, 0.0).astype(jnp.float32)
        + jnp.eye(node_count, dtype=jnp.float32)[None]
    )
    for repeat in range(max(1, (node_count - 1).bit_length())):
        closure = jnp.minimum(
            closure + jnp.einsum("rij,rjk->rik", closure, closure, precision=lax.Precision.HIGHEST),
            1.0,
        )
    return closure > 0.5


def absorb(softmax_state, grouped, keys_vals, valid):
    running_max, denominator, weighted = softmax_state
    head_size = grouped.shape[-1]
    scores = jnp.einsum(
        "rthd,rnd->rthn", grouped, keys_vals[..., :head_size], preferred_element_type=jnp.float32
    ) * head_size ** (-0.5)
    if valid is not None:
        scores = jnp.where(valid[:, :, None, :], scores, neg_large)
    new_max = jnp.maximum(running_max, jnp.max(scores, axis=-1))
    weights = jnp.exp(scores - new_max[..., None])
    if valid is not None:
        weights = jnp.where(valid[:, :, None, :], weights, 0.0)
    factor = jnp.exp(running_max - new_max)
    denominator = denominator * factor + jnp.sum(weights, axis=-1)
    weighted = weighted * factor[..., None] + jnp.einsum(
        "rthn,rnd->rthd",
        weights.astype(jnp.bfloat16),
        keys_vals[..., head_size:],
        preferred_element_type=jnp.float32,
    )
    return (new_max, denominator, weighted)


def absorb_prompt(softmax_state, grouped, shard_kv, group_ids):
    length = shard_kv.shape[1]
    block_count = length // block_len

    def one_block(running, number):
        block_kv = lax.dynamic_slice_in_dim(shard_kv, number * block_len, block_len, 1)
        chosen = jnp.take(block_kv, group_ids, axis=0)
        return (absorb(running, grouped, chosen, None), None)

    softmax_state, unused = lax.scan(
        one_block, softmax_state, jnp.arange(block_count, dtype=jnp.int32)
    )
    return softmax_state


def local(
    queries, tree_kv, suffix_kv, suffix_len, group_ids, parents, accepted, prompt_kv, out_weight
):
    requests, node_count = parents.shape
    pair_width = tree_kv.shape[1]
    head_size = pair_width // 2
    head_count = queries.shape[1] // head_size
    grouped = queries.reshape(requests, node_count, head_count, head_size)
    own_keys = tree_kv.reshape(requests, node_count, pair_width)
    start_state = (
        jnp.full((requests, node_count, head_count), neg_large, jnp.float32),
        jnp.zeros((requests, node_count, head_count), jnp.float32),
        jnp.zeros((requests, node_count, head_count, head_size), jnp.float32),
    )
    softmax_state = absorb(start_state, grouped, own_keys, ancestry(parents))
    slot_count = suffix_kv.shape[1]
    used_slots = jnp.arange(slot_count, dtype=jnp.int32)[None, None, :] < suffix_len[:, None, None]
    softmax_state = absorb(softmax_state, grouped, suffix_kv, used_slots)
    softmax_state = absorb_prompt(
        softmax_state, grouped, lax.all_gather(prompt_kv, "req", axis=1, tiled=True), group_ids
    )
    running_max, denominator, weighted = softmax_state
    attended = (
        (weighted / denominator[..., None])
        .astype(jnp.bfloat16)
        .reshape(requests * node_count, head_count * head_size)
    )
    layer_output = lax.psum_scatter(
        jnp.dot(attended, out_weight, preferred_element_type=jnp.float32).astype(jnp.bfloat16),
        "tp",
        scatter_dimension=0,
        tiled=True,
    )
    path_cache = jnp.take_along_axis(own_keys, accepted[:, :, None], axis=1)
    return (layer_output, path_cache)


def solution(mesh):
    return jax.shard_map(
        local,
        mesh=mesh,
        in_specs=(
            P("req", "tp"),
            P("req", None),
            P("req", None, None),
            P("req"),
            P("req"),
            P("req", None),
            P("req", None),
            P(None, "req", None),
            P("tp", None),
        ),
        out_specs=(P(("req", "tp"), None), P("req", None, None)),
        check_vma=False,
    )
```

profile of v0, /device:TPU:1, one launch (start us, length us, event | category | flops | bytes accessed | tf_op | source)
XLA Modules:
  0.0 208.7 jit_solution(16839389815929757451)
XLA Ops:
  7.2 0.7 all-gather.2.cloned.1.call-update
  8.0 1.2 fusion.17
  11.2 0.8 copy.14
  13.4 0.6 fusion.16
  14.0 0.9 fusion.13
  15.3 86.5 %all-gather.2.cloned.1.call-done = bf16[2,4096,256]{2,1,0:T(8,128)(2,1)} async-done(((bf16[2,32,256]{2,1,0:T(8,128)(2,1)}), bf16[2,4096,256]{2,1,0:T(8,128)(2,1)}) %all-gather.2.cloned.1.call-update) | async-done | bytes 4194320 | tf_op jit(solution)/shard_map/all_gather | solution.py:83
  101.9 70.5 %while.14 = (s32[]{:T(128)}, f32[6,64,4]{1,2,0:T(4,128)S(1)}, f32[6,64,4]{1,2,0:T(4,128)S(1)}, f32[6,64,4,128]{3,1,2,0:T(8,128)S(1)}, s32[6]{0:T(128)S(1)}, /*in...) while((s32[]{:T(128)}, f32[6,64,4]{1,2,0:T(4,128)S(1)}, ...), condition=%wide.region_7.8_spmd, body=%wide.region_4.7_spmd.sunk | while | flops 410128448 | bytes 22004052 | solution.py:58
  103.0 1.1 constant_dynamic-slice_fusion.2
  104.1 1.9 gather_fusion
  106.0 1.7 broadcast_select_fusion.2
  107.7 0.7 bitcast_reduce_fusion.2
  108.4 1.0 fusion.79
  109.4 1.2 fusion.80
  110.7 0.6 dynamic_slice.11
  111.8 1.1 constant_dynamic-slice_fusion.2
  113.0 1.9 gather_fusion
  114.9 1.7 broadcast_select_fusion.2
  116.5 0.7 bitcast_reduce_fusion.2
  117.2 1.0 fusion.79
  118.2 1.2 fusion.80
  119.5 0.6 dynamic_slice.11
  120.7 1.1 constant_dynamic-slice_fusion.2
  121.8 1.9 gather_fusion
  123.7 1.7 broadcast_select_fusion.2
  125.4 0.7 bitcast_reduce_fusion.2
  126.0 1.0 fusion.79
  127.0 1.2 fusion.80
  128.3 0.6 dynamic_slice.11
  129.5 1.1 constant_dynamic-slice_fusion.2
  130.6 1.9 gather_fusion
  132.5 1.7 broadcast_select_fusion.2
  134.2 0.7 bitcast_reduce_fusion.2
  134.9 1.0 fusion.79
  135.9 1.2 fusion.80
  137.1 0.6 dynamic_slice.11
  138.3 1.1 constant_dynamic-slice_fusion.2
  139.4 1.9 gather_fusion
  141.3 1.7 broadcast_select_fusion.2
  143.0 0.7 bitcast_reduce_fusion.2
  143.7 1.0 fusion.79
  144.7 1.2 fusion.80
  147.1 1.1 constant_dynamic-slice_fusion.2
  148.2 1.9 gather_fusion
  150.1 1.7 broadcast_select_fusion.2
  151.8 0.7 bitcast_reduce_fusion.2
  152.5 1.0 fusion.79
  153.5 1.2 fusion.80
  155.9 1.1 constant_dynamic-slice_fusion.2
  157.0 1.9 gather_fusion
  158.9 1.7 broadcast_select_fusion.2
  160.6 0.7 bitcast_reduce_fusion.2
  161.3 1.0 fusion.79
  162.3 1.2 fusion.80
  164.7 1.1 constant_dynamic-slice_fusion.2
  165.9 1.9 gather_fusion
  167.8 1.7 broadcast_select_fusion.2
  169.4 0.7 bitcast_reduce_fusion.2
  170.1 1.0 fusion.79
  171.1 1.2 fusion.80
  173.0 2.2 %convolution_convert_fusion = bf16[384,2048]{1,0:T(8,128)(2,1)} fusion(bf16[512,2048]{1,0:T(8,128)(2,1)S(1)} %copy-done, bf16[48,8,4,128]{3,2,1,0:T(4,128)(2,1)S(1)} %bitcast.122), kind=kOutput, calls=%fused_computation.24 | convolution fusion | flops 806092800 | bytes 4063232 | tf_op jit(solution)/shard_map/dot_general | solution.py:92
  175.2 0.7 copy-done.7
  176.1 1.0 gather_fusion.1
  177.1 0.7 bitcast_select_fusion
  177.8 24.0 %reduce-scatter.2.cloned.1.call-done = bf16[96,2048]{1,0:T(8,128)(2,1)} async-done(((bf16[384,2048]{1,0:T(8,128)(2,1)}), bf16[96,2048]{1,0:T(8,128)(2,1)}) %reduce-scatter.2.cloned.1.call-update) | async-done | bytes 393232 | tf_op jit(solution)/shard_map/reduce_scatter | solution.py:91
  (110 shorter events, 7.3 us)
Async XLA Ops:
  7.2 165.8 %copy-start = (bf16[512,2048]{1,0:T(8,128)(2,1)S(1)}, bf16[512,2048]{1,0:T(8,128)(2,1)}, u32[]{:S(2)}) copy-start(bf16[512,2048]{1,0:T(8,128)(2,1)} %param.19) | copy-start | bytes 6291460
  7.2 94.7 %all-gather.2.cloned.1.call-start = ((), (), s32[]{:S(2)}) async-start(), calls=%async_computation.1 | async-start | bytes 4227072 | tf_op jit(solution)/shard_map/all_gather | solution.py:83
  7.9 193.9 %reduce-scatter.2.cloned.1.call-start = ((), (), s32[]{:S(2)}) async-start(), calls=%async_computation.2 | async-start | bytes 1966080 | tf_op jit(solution)/shard_map/reduce_scatter | solution.py:91
  8.0 3.1 %copy-start.4 = (bf16[384,512]{1,0:T(8,128)(2,1)S(1)}, bf16[384,512]{1,0:T(8,128)(2,1)}, u32[]{:S(2)}) copy-start(bf16[384,512]{1,0:T(8,128)(2,1)} %param.11) | copy-start | bytes 1179652
  9.9 2.1 %copy-start.8 = (s32[6]{0:T(128)S(1)}, s32[6]{0:T(128)}, u32[]{:S(2)}) copy-start(s32[6]{0:T(128)} %param.14) | copy-start | bytes 76
  9.9 2.2 %copy-start.2 = (bf16[384,256]{1,0:T(8,128)(2,1)S(1)}, bf16[384,256]{1,0:T(8,128)(2,1)}, u32[]{:S(2)}) copy-start(bf16[384,256]{1,0:T(8,128)(2,1)} %param.12) | copy-start | bytes 589828
  11.2 1.5 copy-start.5
  13.4 1.5 copy-start.6
  14.9 87.0 %copy-start.9 = (s32[6]{0:T(128)S(1)}, s32[6]{0:T(128)}, u32[]{:S(2)}) copy-start(s32[6]{0:T(128)} %param.15) | copy-start | bytes 76
  106.0 1.7 copy-start.1
  114.9 1.7 copy-start.1
  123.7 1.7 copy-start.1
  132.5 1.7 copy-start.1
  141.3 1.7 copy-start.1
  150.1 1.7 copy-start.1
  158.9 1.7 copy-start.1
  167.8 1.7 copy-start.1
  175.2 0.7 copy-start.7
  175.2 0.9 copy-start.3
Sparse Core Ops, SparseCore 0:
  11.2 90.6 all-gather.1
  175.3 26.4 reduce-scatter.1
where the time goes:
time: 209 us
  waiting for transfers between devices  111 us (53%)
  local copies, waits for them, and re-layouts  31.9 us (15%)
  other arithmetic  23.4 us (11%)
  matrix products  22.5 us (11%)
  between operations  14.3 us (7%)
  loops' own time  5.25 us (3%)
    all_gather x1, waiting for transfers between devices, local(): lax.all_gather(prompt_kv, 'req', axis=1, tiled=True)  86.5 us
    reduce_scatter x1, waiting for transfers between devices, local(): lax.psum_scatter(jnp.dot(attended, out_weight, preferred_element_type=jnp...  24 us
    gather x8, local copies, waits for them, and re-layouts, one_block(): chosen = jnp.take(block_kv, group_ids, axis=0)  15.2 us
    select_n x16, other arithmetic, one_block(): chosen = jnp.take(block_kv, group_ids, axis=0)  13.4 us
    dot_general x10, matrix products, absorb(): jnp.einsum('rthn,rnd->rthd', weights.astype(jnp.bfloat16), keys_vals[...,...  11.3 us
    dynamic_slice x8, local copies, waits for them, and re-layouts, one_block(): lax.dynamic_slice_in_dim(shard_kv, number * block_len, block_len, 1)  8.68 us
    reduce_sum x10, other arithmetic, absorb(): denominator = denominator * factor + jnp.sum(weights, axis=-1)  8.67 us
    dot_general x10, matrix products, absorb(): jnp.einsum('rthd,rnd->rthn', grouped, keys_vals[..., :head_size], preferr...  6.25 us
  transfers between devices with their start and end apart: 2, of which 2 were waited for; matrix products, arithmetic and copies ran while one was open for 4% of the time, Pallas kernels for 0%

commit v1 on v0

v1 whole, which is shorter than its diff:
```python
import functools
import math

import jax
import jax.numpy as jnp
from jax import lax
from jax.experimental import pallas as pl
from jax.experimental.pallas import tpu as pltpu
from jax.sharding import PartitionSpec as P

MESH = pl.DeviceIdType.MESH
ring = 8
hd = 128
neg_large = -1e30
bf16 = jnp.bfloat16
f32 = jnp.float32


def dot(a, b):
    return jnp.dot(a, b, preferred_element_type=f32)


def dot_nt(a, b):
    return lax.dot_general(a, b, (((1,), (1,)), ((), ())), preferred_element_type=f32)


def dot_tn(a, b):
    return lax.dot_general(a, b, (((0,), (0,)), ((), ())), preferred_element_type=f32)


def kernel(
    len_ref, group_ref, parents_ref, accepted_ref, q_hbm, tree_hbm, suf_hbm, prompt_hbm, w_hbm,
    out_ref, path_ref,
    q_ref, tree_ref, suf_ref, w_ref, vt_ref, m_ref, acc_ref, part, half_in, full_in,
    local_sem, p1_send, p1_recv, p2_send, p2_recv, x_send, x_recv, rs_send, rs_recv, *prompt_refs,
):
    requests, nodes = parents_ref.shape
    heads = q_ref.shape[1] // hd
    cols = nodes * heads
    shard = prompt_hbm.shape[1]
    blk = ring * shard
    half = blk // 2
    mine, theirs = prompt_refs[:ring], prompt_refs[ring:]
    scale = math.log2(math.e) / math.sqrt(hd)

    me = lax.axis_index("req")
    tp = lax.axis_index("tp")
    core = lax.rem(me, 2)
    y = lax.rem(me // 2, ring)
    z = me // (2 * ring)

    def along(g, step):
        if g == 0:
            return (z * ring + lax.rem(y + step, ring)) * 2 + core
        return (lax.rem(z + step, ring) * ring + y) * 2 + core

    other = me + 1 - 2 * core
    right = lax.rem(tp + 1, 4)
    left = lax.rem(tp + 3, 4)

    locals_ = [
        pltpu.make_async_copy(prompt_hbm.at[0], mine[0].at[0, pl.ds(0, shard)], local_sem.at[0]),
        pltpu.make_async_copy(prompt_hbm.at[1], mine[0].at[1, pl.ds(0, shard)], local_sem.at[1]),
        pltpu.make_async_copy(q_hbm, q_ref, local_sem.at[2]),
        pltpu.make_async_copy(tree_hbm, tree_ref, local_sem.at[3]),
        pltpu.make_async_copy(suf_hbm, suf_ref, local_sem.at[4]),
        pltpu.make_async_copy(w_hbm, w_ref, local_sem.at[5]),
    ]
    for copy in locals_:
        copy.start()

    barrier = pltpu.get_barrier_semaphore()
    for g in (0, 1):
        for step in range(1, ring):
            pl.semaphore_signal(barrier, inc=1, device_id=(along(g, step), tp), device_id_type=MESH)
    pl.semaphore_signal(barrier, inc=1, device_id=(other, tp), device_id_type=MESH)
    pl.semaphore_signal(barrier, inc=1, device_id=(me, right), device_id_type=MESH)
    pl.semaphore_signal(barrier, inc=1, device_id=(me, left), device_id_type=MESH)
    pl.semaphore_wait(barrier, 2 * (ring - 1) + 3)

    def phase1(g, step):
        return pltpu.make_async_remote_copy(
            src_ref=prompt_hbm.at[g],
            dst_ref=mine[0].at[g, pl.ds(step * shard, shard)],
            send_sem=p1_send.at[g, step],
            recv_sem=p1_recv.at[g, step],
            device_id=(along(g, step), tp),
            device_id_type=MESH,
        )

    def phase2(g, slot, h):
        if slot < 4 or (slot == 4 and h == 0):
            source, target = slot - 1, along(1 - g, 1)
        else:
            source, target = (slot + 1) % ring, along(1 - g, ring - 1)
        return pltpu.make_async_remote_copy(
            src_ref=mine[source].at[g, pl.ds(h * half, half)],
            dst_ref=mine[slot].at[g, pl.ds(h * half, half)],
            send_sem=p2_send.at[g, slot, h],
            recv_sem=p2_recv.at[g, slot, h],
            device_id=(target, tp),
            device_id_type=MESH,
        )

    def exchange(g, slot, h):
        return pltpu.make_async_remote_copy(
            src_ref=mine[slot].at[g, pl.ds(h * half, half)],
            dst_ref=theirs[slot].at[g, pl.ds(h * half, half)],
            send_sem=x_send.at[g, slot, h],
            recv_sem=x_recv.at[g, slot, h],
            device_id=(other, tp),
            device_id_type=MESH,
        )

    started = []

    def start(copy):
        copy.start()
        started.append(copy)

    for step in (1, 7, 2, 6, 3, 5, 4):
        for g in (0, 1):
            start(phase1(g, step))

    eye = jnp.where(
        lax.broadcasted_iota(jnp.int32, (hd, hd), 0) == lax.broadcasted_iota(jnp.int32, (hd, hd), 1),
        1.0, 0.0,
    ).astype(bf16)

    def values_t(values):
        turned = dot_nt(eye, values).astype(bf16)
        return jnp.concatenate([turned, jnp.ones((16, values.shape[0]), bf16)], axis=0)

    def query(r):
        rows = pl.ds(pl.multiple_of(r * nodes, nodes), nodes)
        return jnp.concatenate(
            [q_ref[rows, h * hd : (h + 1) * hd] for h in range(heads)], axis=0
        )

    locals_[2].wait()
    locals_[3].wait()
    locals_[4].wait()

    row = lax.broadcasted_iota(jnp.int32, (nodes, nodes), 0)
    col = lax.broadcasted_iota(jnp.int32, (nodes, nodes), 1)
    spread = jnp.where(
        lax.broadcasted_iota(jnp.int32, (nodes, cols), 0)
        == lax.rem(lax.broadcasted_iota(jnp.int32, (nodes, cols), 1), nodes),
        1.0, 0.0,
    ).astype(bf16)
    node_path = lax.broadcasted_iota(jnp.int32, (nodes, accepted_ref.shape[1]), 0)
    closures = []
    for r in range(requests):
        up = (parents_ref[r : r + 1, :] == row) & (col > 0)
        closures.append(jnp.where(up | (row == col), 1.0, 0.0).astype(bf16))
    for repeat in range((nodes - 1).bit_length()):
        closures = [jnp.minimum(dot(c, c), 1.0).astype(bf16) for c in closures]
    slots = lax.broadcasted_iota(jnp.int32, (suf_ref.shape[1], cols), 0)
    for r in range(requests):
        related = dot(closures[r], spread) > 0.5
        tree = tree_ref[r * nodes : (r + 1) * nodes, :]
        q = query(r)
        s0 = jnp.where(related, dot_nt(tree[:, :hd], q), neg_large)
        s1 = jnp.where(slots < len_ref[r], dot_nt(suf_ref[r, :, :hd], q), neg_large)
        top = jnp.maximum(
            jnp.max(s0, axis=0, keepdims=True), jnp.max(s1, axis=0, keepdims=True)
        )
        p0 = jnp.exp2((s0 - top) * scale).astype(bf16)
        p1 = jnp.exp2((s1 - top) * scale).astype(bf16)
        m_ref[r] = top
        acc_ref[r] = dot(values_t(tree[:, hd:]), p0) + dot(values_t(suf_ref[r, :, hd:]), p1)
        chosen = jnp.where(node_path == accepted_ref[r : r + 1, :], 1.0, 0.0).astype(bf16)
        path_ref[r] = dot_tn(chosen, tree).astype(bf16)

    def absorb(pieces):
        for block in pieces:
            for g in (0, 1):
                vt_ref[block, g] = values_t(prompt_refs[block][g, :, hd:])

        def one(r):
            g = group_ref[r]
            q = query(r)
            scores = [dot_nt(prompt_refs[block][g, :, :hd], q) for block in pieces]
            before = m_ref[r]
            top = before
            for s in scores:
                top = jnp.maximum(top, jnp.max(s, axis=0, keepdims=True))
            total = acc_ref[r] * jnp.exp2((before - top) * scale)
            for s, block in zip(scores, pieces):
                weights = jnp.exp2((s - top) * scale).astype(bf16)
                total = total + dot(vt_ref[block, g], weights)
            m_ref[r] = top
            acc_ref[r] = total

        def body(pair, carry):
            one(2 * pair)
            one(2 * pair + 1)
            return carry

        lax.fori_loop(0, requests // 2, body, 0)

    locals_[0].wait()
    locals_[1].wait()
    for step in range(1, ring):
        for g in (0, 1):
            phase1(g, step).wait_recv()

    for h in (0, 1):
        for slot in (1, 7):
            for g in (0, 1):
                start(phase2(g, slot, h))
        for g in (0, 1):
            start(exchange(g, 0, h))
    for h in (0, 1):
        for g in (0, 1):
            exchange(g, 0, h).wait_recv()
    absorb([0, ring])

    for k in (1, 2, 3):
        for h in (0, 1):
            for slot in (k, ring - k):
                for g in (0, 1):
                    phase2(g, slot, h).wait_recv()
                    after = slot + 1 if slot < 4 else slot - 1
                    if after != 4 or (slot == 3) == (h == 0):
                        start(phase2(g, after, h))
                    start(exchange(g, slot, h))
        for h in (0, 1):
            for slot in (k, ring - k):
                for g in (0, 1):
                    exchange(g, slot, h).wait_recv()
        absorb([k, ring + k, ring - k, 2 * ring - k])
    for h in (0, 1):
        for g in (0, 1):
            phase2(g, 4, h).wait_recv()
            start(exchange(g, 4, h))
    for h in (0, 1):
        for g in (0, 1):
            exchange(g, 4, h).wait_recv()
    absorb([4, ring + 4])

    locals_[5].wait()

    def finish(r, carry):
        total = acc_ref[r]
        turned = (total[:hd] / total[hd : hd + 1]).T.astype(bf16)
        attended = jnp.concatenate(
            [turned[h * nodes : (h + 1) * nodes] for h in range(heads)], axis=1
        )
        rows = pl.ds(pl.multiple_of(r * nodes, nodes), nodes)
        part[rows, :] = dot(attended, w_ref[...]).astype(bf16)
        return carry

    lax.fori_loop(0, requests, finish, 0)

    rows_out = out_ref.shape[0]
    rows_half = rows_out // 2

    def block(device, h=None):
        if h is None:
            return pl.ds(pl.multiple_of(device * rows_out, 16), rows_out)
        return pl.ds(pl.multiple_of(device * rows_out + h * rows_half, 16), rows_half)

    across = lax.rem(tp + 2, 4)
    sides = (right, left)

    def scatter(stage, way):
        if stage == 0:
            source, target = part.at[block(across, way)], half_in.at[way]
        else:
            h = way if stage == 2 else 1 - way
            source = part.at[block(sides[way], h)]
            target = full_in.at[way, pl.ds(h * rows_half, rows_half)]
        return pltpu.make_async_remote_copy(
            src_ref=source,
            dst_ref=target,
            send_sem=rs_send.at[stage, way],
            recv_sem=rs_recv.at[stage, way],
            device_id=(me, sides[way]),
            device_id_type=MESH,
        )

    for stage in (0, 1):
        for way in (0, 1):
            start(scatter(stage, way))
    for way in (0, 1):
        scatter(0, way).wait_recv()
        rows = block(sides[way], way)
        part[rows, :] = (part[rows, :].astype(f32) + half_in[way].astype(f32)).astype(bf16)
        start(scatter(2, way))
    for stage in (1, 2):
        for way in (0, 1):
            scatter(stage, way).wait_recv()
    out_ref[...] = (
        part[block(tp), :].astype(f32) + full_in[0].astype(f32) + full_in[1].astype(f32)
    ).astype(bf16)
    for copy in started:
        copy.wait_send()


def local(
    queries, tree_kv, suffix_kv, suffix_len, group_ids, parents, accepted, prompt_kv, out_weight
):
    requests, nodes = parents.shape
    groups, shard, width = prompt_kv.shape
    heads = queries.shape[1] // hd
    cols = nodes * heads
    rows_out = queries.shape[0] // 4
    model = out_weight.shape[1]
    anywhere = pl.BlockSpec(memory_space=pl.ANY)
    smem = pl.BlockSpec(memory_space=pltpu.SMEM)
    vmem = pl.BlockSpec(memory_space=pltpu.VMEM)
    dma = pltpu.SemaphoreType.DMA
    return pl.pallas_call(
        kernel,
        out_shape=(
            jax.ShapeDtypeStruct((rows_out, model), bf16),
            jax.ShapeDtypeStruct((requests, accepted.shape[1], width), bf16),
        ),
        in_specs=[smem, smem, vmem, vmem] + [anywhere] * 5,
        out_specs=(vmem, vmem),
        scratch_shapes=[
            pltpu.VMEM(queries.shape, bf16),
            pltpu.VMEM(tree_kv.shape, bf16),
            pltpu.VMEM(suffix_kv.shape, bf16),
            pltpu.VMEM(out_weight.shape, bf16),
            pltpu.VMEM((2 * ring, groups, hd + 16, ring * shard), bf16),
            pltpu.VMEM((requests, 1, cols), f32),
            pltpu.VMEM((requests, hd + 16, cols), f32),
            pltpu.VMEM((queries.shape[0], model), bf16),
            pltpu.VMEM((2, rows_out // 2, model), bf16),
            pltpu.VMEM((2, rows_out, model), bf16),
            dma((6,)),
            dma((2, ring)),
            dma((2, ring)),
            dma((2, ring, 2)),
            dma((2, ring, 2)),
            dma((2, ring, 2)),
            dma((2, ring, 2)),
            dma((3, 2)),
            dma((3, 2)),
        ]
        + [pltpu.VMEM((groups, ring * shard, width), bf16)] * (2 * ring),
        compiler_params=pltpu.CompilerParams(
            collective_id=0, has_side_effects=True, vmem_limit_bytes=48 << 20
        ),
        name="verify_attention",
    )(
        suffix_len, group_ids, parents, accepted, queries, tree_kv, suffix_kv, prompt_kv, out_weight
    )


def solution(mesh):
    return jax.shard_map(
        local,
        mesh=mesh,
        in_specs=(
            P("req", "tp"),
            P("req", None),
            P("req", None, None),
            P("req"),
            P("req"),
            P("req", None),
            P("req", None),
            P(None, "req", None),
            P("tp", None),
        ),
        out_specs=(P(("req", "tp"), None), P("req", None, None)),
        check_vma=False,
    )
```

time: 209 us -> 77.2 us (0.37)
  waiting for transfers between devices: 111 us -> 0 us
  Pallas kernels: 0 us -> 66.7 us
  other arithmetic: 23.4 us -> 0 us
  matrix products: 22.5 us -> 0 us
  local copies, waits for them, and re-layouts: 31.9 us -> 9.43 us
  between operations: 14.3 us -> 0.66 us
  loops' own time: 5.25 us -> 0 us
    all_gather x1 -> x0, waiting for transfers between devices: 86.5 us -> none  [local(): lax.all_gather(prompt_kv, 'req', axis=1, tiled=True)]
    pallas_call x0 -> x1, Pallas kernels: none -> 66.7 us  [local(): pl.pallas_call(kernel, out_shape=(jax.ShapeDtypeStruct((rows_out, model),...]
    reduce_scatter x1 -> x0, waiting for transfers between devices: 24 us -> none  [local(): lax.psum_scatter(jnp.dot(attended, out_weight, preferred_element_type=jnp...]
    dot_general x27 -> x0, matrix products: 22.5 us -> none  [the longest x10 11.3 us: absorb(): jnp.einsum('rthn,rnd->rthd', weights.astype(jnp.bfloat16), keys_vals[...,...]
    gather x10 -> x0, local copies, waits for them, and re-layouts: 16.2 us -> none  [the longest x8 15.2 us: one_block(): chosen = jnp.take(block_kv, group_ids, axis=0)]
    select_n x17 -> x0, other arithmetic: 14.1 us -> none  [the longest x16 13.4 us: one_block(): chosen = jnp.take(block_kv, group_ids, axis=0)]
    dynamic_slice x16 -> x0, local copies, waits for them, and re-layouts: 13.3 us -> none  [the longest x8 8.68 us: one_block(): lax.dynamic_slice_in_dim(shard_kv, number * block_len, block_len, 1)]
    reduce_sum x10 -> x0, other arithmetic: 8.67 us -> none  [absorb(): denominator = denominator * factor + jnp.sum(weights, axis=-1)]
  transfers between devices with their start and end apart: 2 -> 0, of which waited for: 2 -> 0; matrix products, arithmetic and copies ran while one was open for 4% -> 0% of each run, Pallas kernels for 0% -> 0%
where the time goes in v1:
time: 77.2 us; the launch traced here: 76.8 us
  Pallas kernels  66.7 us (86%)
  local copies, waits for them, and re-layouts  9.43 us (12%)
    pallas_call x1, Pallas kernels, local(): pl.pallas_call(kernel, out_shape=(jax.ShapeDtypeStruct((rows_out, model),...  66.7 us
    unnamed x20, local copies, waits for them, and re-layouts  9.43 us

profile of v1, /device:TPU:1, one launch (start us, length us, event | category | flops | bytes accessed | tf_op | source)
XLA Modules:
  0.0 76.8 jit_solution(7186898196121991356)
XLA Ops:
  0.6 0.0 copy-start
  0.6 1.6 %copy-done = bf16[512,2048]{1,0:T(8,128)(2,1)S(1)} copy-done((bf16[512,2048]{1,0:T(8,128)(2,1)S(1)}, bf16[512,2048]{1,0:T(8,128)(2,1)}, u32[]{:S(2)}) %copy-start) | copy-done | bytes 2097176
  2.2 0.0 copy-start.1
  2.2 1.1 %copy-done.1 = bf16[6,256,256]{2,1,0:T(8,128)(2,1)S(1)} copy-done((bf16[6,256,256]{2,1,0:T(8,128)(2,1)S(1)}, bf16[6,256,256]{2,1,0:T(8,128)(2,1)}, u32[]{:S(2)}) %copy-start.1) | copy-done | bytes 786456
  3.4 0.0 copy-start.2
  3.4 1.0 %copy-done.2 = bf16[384,512]{1,0:T(8,128)(2,1)S(1)} copy-done((bf16[384,512]{1,0:T(8,128)(2,1)S(1)}, bf16[384,512]{1,0:T(8,128)(2,1)}, u32[]{:S(2)}) %copy-start.2) | copy-done | bytes 393240
  4.4 0.0 copy-start.3
  4.4 0.9 %copy-done.3 = bf16[384,256]{1,0:T(8,128)(2,1)S(1)} copy-done((bf16[384,256]{1,0:T(8,128)(2,1)S(1)}, bf16[384,256]{1,0:T(8,128)(2,1)}, u32[]{:S(2)}) %copy-start.3) | copy-done | bytes 196632
  5.3 0.0 copy-start.4
  5.3 0.8 copy-done.4
  6.0 0.0 copy-start.5
  6.0 0.7 copy-done.5
  6.7 0.0 copy-start.6
  6.7 0.7 copy-done.6
  7.4 0.0 copy-start.7
  7.4 0.7 copy-done.7
  8.1 0.0 copy-start.8
  8.1 0.7 copy-done.8
  8.7 66.7 %verify_attention.1 = (bf16[96,2048]{1,0:T(8,128)(2,1)S(1)}, bf16[6,8,256]{2,1,0:T(8,128)(2,1)S(1)}) custom-call(s32[6]{0:T(128)S(1)} %copy-done.7, s32[6]{0:T(128)S(1)} %copy-done.8, s32[6,64]{1,0:T(8,128)S(1)} %copy-done.5, s32[6,8]{1,0:T(8,128)S(1)} %copy-done.6, bf16[384,512]{1,0:T(8,128)(2,1)S(1)} %copy-done.2, bf16[384,256]{1,0:T(8,128)(2,1)S(1)} %copy-done.3, ...), custom_call_target="tpu_custom_call" | custom-call | tf_op jit(solution)/shard_map/verify_attention/pallas_call | solution.py:314
  75.4 0.7 copy.13
  76.2 0.6 copy.14
Async XLA Ops:
  0.6 1.6 %copy-start = (bf16[512,2048]{1,0:T(8,128)(2,1)S(1)}, bf16[512,2048]{1,0:T(8,128)(2,1)}, u32[]{:S(2)}) copy-start(bf16[512,2048]{1,0:T(8,128)(2,1)} %w_hbm.1) | copy-start | bytes 6291460
  2.2 1.1 %copy-start.1 = (bf16[6,256,256]{2,1,0:T(8,128)(2,1)S(1)}, bf16[6,256,256]{2,1,0:T(8,128)(2,1)}, u32[]{:S(2)}) copy-start(bf16[6,256,256]{2,1,0:T(8,128)(2,1)} %suf_hbm.1) | copy-start | bytes 2359300
  3.4 1.0 %copy-start.2 = (bf16[384,512]{1,0:T(8,128)(2,1)S(1)}, bf16[384,512]{1,0:T(8,128)(2,1)}, u32[]{:S(2)}) copy-start(bf16[384,512]{1,0:T(8,128)(2,1)} %q_hbm.1) | copy-start | bytes 1179652
  4.4 0.9 %copy-start.3 = (bf16[384,256]{1,0:T(8,128)(2,1)S(1)}, bf16[384,256]{1,0:T(8,128)(2,1)}, u32[]{:S(2)}) copy-start(bf16[384,256]{1,0:T(8,128)(2,1)} %tree_hbm.1) | copy-start | bytes 589828
  5.3 0.8 copy-start.4
  6.0 0.7 copy-start.5
  6.7 0.7 copy-start.6
  7.4 0.7 copy-start.7
  8.1 0.7 copy-start.8

commit v2 on v1

--- a/solution.py
+++ b/solution.py
@@ -29,9 +29,9 @@
 
 
 def kernel(
-    len_ref, group_ref, parents_ref, accepted_ref, q_hbm, tree_hbm, suf_hbm, prompt_hbm, w_hbm,
+    len_hbm, group_hbm, parents_hbm, accepted_hbm, q_hbm, tree_hbm, suf_hbm, prompt_hbm, w_hbm,
     out_ref, path_ref,
-    q_ref, tree_ref, suf_ref, w_ref, vt_ref, m_ref, acc_ref, part, half_in, full_in,
+    len_ref, group_ref, parents_ref, accepted_ref, q_ref, tree_ref, suf_ref, w_ref, vt_ref, m_ref, acc_ref, part, half_in, full_in,
     local_sem, p1_send, p1_recv, p2_send, p2_recv, x_send, x_recv, rs_send, rs_recv, *prompt_refs,
 ):
     requests, nodes = parents_ref.shape
@@ -65,6 +65,10 @@
         pltpu.make_async_copy(tree_hbm, tree_ref, local_sem.at[3]),
         pltpu.make_async_copy(suf_hbm, suf_ref, local_sem.at[4]),
         pltpu.make_async_copy(w_hbm, w_ref, local_sem.at[5]),
+        pltpu.make_async_copy(len_hbm, len_ref, local_sem.at[6]),
+        pltpu.make_async_copy(group_hbm, group_ref, local_sem.at[7]),
+        pltpu.make_async_copy(parents_hbm, parents_ref, local_sem.at[8]),
+        pltpu.make_async_copy(accepted_hbm, accepted_ref, local_sem.at[9]),
     ]
     for copy in locals_:
         copy.start()
@@ -137,9 +141,8 @@
             [q_ref[rows, h * hd : (h + 1) * hd] for h in range(heads)], axis=0
         )
 
-    locals_[2].wait()
-    locals_[3].wait()
-    locals_[4].wait()
+    for number in (2, 3, 4, 6, 7, 8, 9):
+        locals_[number].wait()
 
     row = lax.broadcasted_iota(jnp.int32, (nodes, nodes), 0)
     col = lax.broadcasted_iota(jnp.int32, (nodes, nodes), 1)
@@ -172,32 +175,38 @@
         chosen = jnp.where(node_path == accepted_ref[r : r + 1, :], 1.0, 0.0).astype(bf16)
         path_ref[r] = dot_tn(chosen, tree).astype(bf16)
 
-    def absorb(pieces):
+    def scores_of(pieces, r):
+        g = group_ref[r]
+        q = query(r)
+        return [dot_nt(prompt_refs[block][g, :, :hd], q) for block in pieces]
+
+    def update(pieces, r, scores):
+        g = group_ref[r]
+        before = m_ref[r]
+        top = before
+        for s in scores:
+            top = jnp.maximum(top, jnp.max(s, axis=0, keepdims=True))
+        total = acc_ref[r] * jnp.exp2((before - top) * scale)
+        for s, block in zip(scores, pieces):
+            weights = jnp.exp2((s - top) * scale).astype(bf16)
+            total = total + dot(vt_ref[block, g], weights)
+        return top, total
+
+    def absorb(pieces, order=tuple(range(requests)), done=None):
         for block in pieces:
             for g in (0, 1):
                 vt_ref[block, g] = values_t(prompt_refs[block][g, :, hd:])
-
-        def one(r):
-            g = group_ref[r]
-            q = query(r)
-            scores = [dot_nt(prompt_refs[block][g, :, :hd], q) for block in pieces]
-            before = m_ref[r]
-            top = before
-            for s in scores:
-                top = jnp.maximum(top, jnp.max(s, axis=0, keepdims=True))
-            total = acc_ref[r] * jnp.exp2((before - top) * scale)
-            for s, block in zip(scores, pieces):
-                weights = jnp.exp2((s - top) * scale).astype(bf16)
-                total = total + dot(vt_ref[block, g], weights)
-            m_ref[r] = top
-            acc_ref[r] = total
-
-        def body(pair, carry):
-            one(2 * pair)
-            one(2 * pair + 1)
-            return carry
-
-        lax.fori_loop(0, requests // 2, body, 0)
+        ahead = scores_of(pieces, order[0])
+        for number, r in enumerate(order):
+            scores = ahead
+            if number + 1 < requests:
+                ahead = scores_of(pieces, order[number + 1])
+            top, total = update(pieces, r, scores)
+            if done is None:
+                m_ref[r] = top
+                acc_ref[r] = total
+            else:
+                done(number, r, total)
 
     locals_[0].wait()
     locals_[1].wait()
@@ -211,12 +220,9 @@
                 start(phase2(g, slot, h))
         for g in (0, 1):
             start(exchange(g, 0, h))
-    for h in (0, 1):
-        for g in (0, 1):
-            exchange(g, 0, h).wait_recv()
-    absorb([0, ring])
-
-    for k in (1, 2, 3):
+    absorb([0])
+
+    def pass_on(k):
         for h in (0, 1):
             for slot in (k, ring - k):
                 for g in (0, 1):
@@ -225,33 +231,30 @@
                     if after != 4 or (slot == 3) == (h == 0):
                         start(phase2(g, after, h))
                     start(exchange(g, slot, h))
-        for h in (0, 1):
-            for slot in (k, ring - k):
+
+    def swapped(*slots):
+        for slot in slots:
+            for h in (0, 1):
                 for g in (0, 1):
                     exchange(g, slot, h).wait_recv()
-        absorb([k, ring + k, ring - k, 2 * ring - k])
+
+    pass_on(1)
+    swapped(0)
+    absorb([ring, 1, 7])
+    pass_on(2)
+    swapped(1, 7)
+    absorb([ring + 1, ring + 7, 2, 6])
+    pass_on(3)
+    swapped(2, 6)
+    absorb([ring + 2, ring + 6, 3, 5])
     for h in (0, 1):
         for g in (0, 1):
             phase2(g, 4, h).wait_recv()
             start(exchange(g, 4, h))
-    for h in (0, 1):
-        for g in (0, 1):
-            exchange(g, 4, h).wait_recv()
-    absorb([4, ring + 4])
-
+    swapped(3, 5)
+    absorb([ring + 3, ring + 5, 4])
+    swapped(4)
     locals_[5].wait()
-
-    def finish(r, carry):
-        total = acc_ref[r]
-        turned = (total[:hd] / total[hd : hd + 1]).T.astype(bf16)
-        attended = jnp.concatenate(
-            [turned[h * nodes : (h + 1) * nodes] for h in range(heads)], axis=1
-        )
-        rows = pl.ds(pl.multiple_of(r * nodes, nodes), nodes)
-        part[rows, :] = dot(attended, w_ref[...]).astype(bf16)
-        return carry
-
-    lax.fori_loop(0, requests, finish, 0)
 
     rows_out = out_ref.shape[0]
     rows_half = rows_out // 2
@@ -262,30 +265,53 @@
         return pl.ds(pl.multiple_of(device * rows_out + h * rows_half, 16), rows_half)
 
     across = lax.rem(tp + 2, 4)
-    sides = (right, left)
 
     def scatter(stage, way):
+        side = lax.rem(tp + 1 + 2 * way, 4)
         if stage == 0:
             source, target = part.at[block(across, way)], half_in.at[way]
         else:
             h = way if stage == 2 else 1 - way
-            source = part.at[block(sides[way], h)]
-            target = full_in.at[way, pl.ds(h * rows_half, rows_half)]
+            source = part.at[block(side, h)]
+            target = full_in.at[way, pl.ds(pl.multiple_of(h * rows_half, 16), rows_half)]
         return pltpu.make_async_remote_copy(
             src_ref=source,
             dst_ref=target,
             send_sem=rs_send.at[stage, way],
             recv_sem=rs_recv.at[stage, way],
-            device_id=(me, sides[way]),
+            device_id=(me, side),
             device_id_type=MESH,
         )
 
-    for stage in (0, 1):
-        for way in (0, 1):
-            start(scatter(stage, way))
+    odd = lax.rem(tp, 2)
+    near = 1 - odd
+    first = 3 * lax.rem(tp // 2 + 1, 2)
+    second = 3 - first
+    order = (
+        first + 2 * odd, first + 1, first + 2 - 2 * odd,
+        second + 1, second + 2 - 2 * odd, second + 2 * odd,
+    )
+
+    def finish(number, r, total):
+        turned = (total[:hd] * (1.0 / total[hd : hd + 1])).T.astype(bf16)
+        attended = jnp.concatenate(
+            [turned[h * nodes : (h + 1) * nodes] for h in range(heads)], axis=1
+        )
+        rows = pl.ds(pl.multiple_of(r * nodes, nodes), nodes)
+        part[rows, :] = dot(attended, w_ref[...]).astype(bf16)
+        if number == 1:
+            for way in (0, 1):
+                start(scatter(0, way))
+        if number == 2:
+            start(scatter(1, near))
+        if number == 4:
+            start(scatter(1, 1 - near))
+
+    absorb([ring + 4], order, finish)
+
     for way in (0, 1):
         scatter(0, way).wait_recv()
-        rows = block(sides[way], way)
+        rows = block(lax.rem(tp + 1 + 2 * way, 4), way)
         part[rows, :] = (part[rows, :].astype(f32) + half_in[way].astype(f32)).astype(bf16)
         start(scatter(2, way))
     for stage in (1, 2):
@@ -307,8 +333,7 @@
     cols = nodes * heads
     rows_out = queries.shape[0] // 4
     model = out_weight.shape[1]
-    anywhere = pl.BlockSpec(memory_space=pl.ANY)
-    smem = pl.BlockSpec(memory_space=pltpu.SMEM)
+    hbm = pl.BlockSpec(memory_space=pltpu.HBM)
     vmem = pl.BlockSpec(memory_space=pltpu.VMEM)
     dma = pltpu.SemaphoreType.DMA
     return pl.pallas_call(
@@ -317,9 +342,13 @@
             jax.ShapeDtypeStruct((rows_out, model), bf16),
             jax.ShapeDtypeStruct((requests, accepted.shape[1], width), bf16),
         ),
-        in_specs=[smem, smem, vmem, vmem] + [anywhere] * 5,
+        in_specs=[hbm] * 9,
         out_specs=(vmem, vmem),
         scratch_shapes=[
+            pltpu.SMEM(suffix_len.shape, jnp.int32),
+            pltpu.SMEM(group_ids.shape, jnp.int32),
+            pltpu.VMEM(parents.shape, jnp.int32),
+            pltpu.VMEM(accepted.shape, jnp.int32),
             pltpu.VMEM(queries.shape, bf16),
             pltpu.VMEM(tree_kv.shape, bf16),
             pltpu.VMEM(suffix_kv.shape, bf16),
@@ -330,7 +359,7 @@
             pltpu.VMEM((queries.shape[0], model), bf16),
             pltpu.VMEM((2, rows_out // 2, model), bf16),
             pltpu.VMEM((2, rows_out, model), bf16),
-            dma((6,)),
+            dma((10,)),
             dma((2, ring)),
             dma((2, ring)),
             dma((2, ring, 2)),
@@ -342,7 +371,7 @@
         ]
         + [pltpu.VMEM((groups, ring * shard, width), bf16)] * (2 * ring),
         compiler_params=pltpu.CompilerParams(
-            collective_id=0, has_side_effects=True, vmem_limit_bytes=48 << 20
+            collective_id=0, has_side_effects=True, vmem_limit_bytes=62 << 20
         ),
         name="verify_attention",
     )(

time: 77.2 us -> 62.2 us (0.81)
  Pallas kernels: 66.7 us -> 57.7 us
  local copies, waits for them, and re-layouts: 9.43 us -> 3.11 us
    pallas_call x1, Pallas kernels: 66.7 us -> 57.7 us  [local(): pl.pallas_call(kernel, out_shape=(jax.ShapeDtypeStruct((rows_out, model),...]
    unnamed x20 -> x2, local copies, waits for them, and re-layouts: 9.43 us -> 3.11 us
where the time goes in v2:
time: 62.2 us; the launch traced here: 61.4 us
  Pallas kernels  57.7 us (93%)
  local copies, waits for them, and re-layouts  3.11 us (5%)
  between operations  0.64 us (1%)
    pallas_call x1, Pallas kernels, local(): pl.pallas_call(kernel, out_shape=(jax.ShapeDtypeStruct((rows_out, model),...  57.7 us
    unnamed x2, local copies, waits for them, and re-layouts  3.11 us

profile of v2, /device:TPU:1, one launch (start us, length us, event | category | flops | bytes accessed | tf_op | source)
XLA Modules:
  0.0 61.4 jit_solution(3021030245464796842)
XLA Ops:
  0.6 57.7 %verify_attention.1 = (bf16[96,2048]{1,0:T(8,128)(2,1)}, bf16[6,8,256]{2,1,0:T(8,128)(2,1)}) custom-call(s32[6]{0:T(128)} %len_hbm.1, s32[6]{0:T(128)} %group_hbm.1, s32[6,64]{1,0:T(8,128)} %parents_hbm.1, s32[6,8]{1,0:T(8,128)} %accepted_hbm.1, bf16[384,512]{1,0:T(8,128)(2,1)} %q_hbm.1, bf16[384,256]{1,0:T(8,128)(2,1)} %tree_hbm.1, ...), custom_call_target="tpu_custom_call" | custom-call | tf_op jit(solution)/shard_map/verify_attention/pallas_call | solution.py:339
  58.3 1.8 %copy.13 = bf16[96,2048]{1,0:T(8,128)(2,1)} copy(bf16[96,2048]{1,0:T(8,128)(2,1)} %get-tuple-element.4) | data formatting | bytes 786432
  60.1 1.3 %copy.14 = bf16[6,8,256]{2,1,0:T(8,128)(2,1)} copy(bf16[6,8,256]{2,1,0:T(8,128)(2,1)} %get-tuple-element.5) | data formatting | bytes 49152

commit v3 on v2

--- a/solution.py
+++ b/solution.py
@@ -10,6 +10,7 @@
 
 MESH = pl.DeviceIdType.MESH
 ring = 8
+places = {0: 0, 1: 1, 7: 2, 2: 3, 6: 4, 3: 5, 5: 6, 4: 7}
 hd = 128
 neg_large = -1e30
 bf16 = jnp.bfloat16
@@ -85,7 +86,7 @@
     def phase1(g, step):
         return pltpu.make_async_remote_copy(
             src_ref=prompt_hbm.at[g],
-            dst_ref=mine[0].at[g, pl.ds(step * shard, shard)],
+            dst_ref=mine[0].at[g, pl.ds(places[step] * shard, shard)],
             send_sem=p1_send.at[g, step],
             recv_sem=p1_recv.at[g, step],
             device_id=(along(g, step), tp),
@@ -122,7 +123,7 @@
         copy.start()
         started.append(copy)
 
-    for step in (1, 7, 2, 6, 3, 5, 4):
+    for step in (4, 3, 5, 6, 2, 1, 7):
         for g in (0, 1):
             start(phase1(g, step))
 
@@ -159,7 +160,22 @@
     for repeat in range((nodes - 1).bit_length()):
         closures = [jnp.minimum(dot(c, c), 1.0).astype(bf16) for c in closures]
     slots = lax.broadcasted_iota(jnp.int32, (suf_ref.shape[1], cols), 0)
+
+    def set_off(h, steps):
+        for step in steps:
+            for g in (0, 1):
+                phase1(g, step).wait_recv()
+        for slot in (1, 7):
+            for g in (0, 1):
+                start(phase2(g, slot, h))
+        for g in (0, 1):
+            start(exchange(g, 0, h))
+
     for r in range(requests):
+        if r == requests // 2:
+            locals_[0].wait()
+            locals_[1].wait()
+            set_off(0, (1, 7, 2))
         related = dot(closures[r], spread) > 0.5
         tree = tree_ref[r * nodes : (r + 1) * nodes, :]
         q = query(r)
@@ -208,29 +224,21 @@
             else:
                 done(number, r, total)
 
-    locals_[0].wait()
-    locals_[1].wait()
-    for step in range(1, ring):
+    def pass_on(k, h):
+        for slot in (k, ring - k):
+            for g in (0, 1):
+                phase2(g, slot, h).wait_recv()
+                after = slot + 1 if slot < 4 else slot - 1
+                if after != 4 or (slot == 3) == (h == 0):
+                    start(phase2(g, after, h))
+        for slot in (k, ring - k):
+            for g in (0, 1):
+                start(exchange(g, slot, h))
+
+    def last(h):
         for g in (0, 1):
-            phase1(g, step).wait_recv()
-
-    for h in (0, 1):
-        for slot in (1, 7):
-            for g in (0, 1):
-                start(phase2(g, slot, h))
-        for g in (0, 1):
-            start(exchange(g, 0, h))
-    absorb([0])
-
-    def pass_on(k):
-        for h in (0, 1):
-            for slot in (k, ring - k):
-                for g in (0, 1):
-                    phase2(g, slot, h).wait_recv()
-                    after = slot + 1 if slot < 4 else slot - 1
-                    if after != 4 or (slot == 3) == (h == 0):
-                        start(phase2(g, after, h))
-                    start(exchange(g, slot, h))
+            phase2(g, 4, h).wait_recv()
+            start(exchange(g, 4, h))
 
     def swapped(*slots):
         for slot in slots:
@@ -238,21 +246,28 @@
                 for g in (0, 1):
                     exchange(g, slot, h).wait_recv()
 
-    pass_on(1)
+    set_off(1, (6, 3, 5, 4))
+    absorb([0])
+    pass_on(1, 0)
     swapped(0)
-    absorb([ring, 1, 7])
-    pass_on(2)
+    absorb([ring])
+    pass_on(1, 1)
+    absorb([1, 7])
+    pass_on(2, 0)
     swapped(1, 7)
-    absorb([ring + 1, ring + 7, 2, 6])
-    pass_on(3)
+    absorb([ring + 1, ring + 7])
+    pass_on(2, 1)
+    absorb([2, 6])
+    pass_on(3, 0)
     swapped(2, 6)
-    absorb([ring + 2, ring + 6, 3, 5])
-    for h in (0, 1):
-        for g in (0, 1):
-            phase2(g, 4, h).wait_recv()
-            start(exchange(g, 4, h))
+    absorb([ring + 2, ring + 6])
+    pass_on(3, 1)
+    absorb([3, 5])
+    last(0)
     swapped(3, 5)
-    absorb([ring + 3, ring + 5, 4])
+    absorb([ring + 3, ring + 5])
+    last(1)
+    absorb([4])
     swapped(4)
     locals_[5].wait()
 
@@ -284,7 +299,6 @@
         )
 
     odd = lax.rem(tp, 2)
-    near = 1 - odd
     first = 3 * lax.rem(tp // 2 + 1, 2)
     second = 3 - first
     order = (
@@ -292,23 +306,29 @@
         second + 1, second + 2 - 2 * odd, second + 2 * odd,
     )
 
+    held = []
+
     def finish(number, r, total):
         turned = (total[:hd] * (1.0 / total[hd : hd + 1])).T.astype(bf16)
-        attended = jnp.concatenate(
+        held.append((r, jnp.concatenate(
             [turned[h * nodes : (h + 1) * nodes] for h in range(heads)], axis=1
-        )
-        rows = pl.ds(pl.multiple_of(r * nodes, nodes), nodes)
-        part[rows, :] = dot(attended, w_ref[...]).astype(bf16)
+        )))
+        if number in (0, 3):
+            return
+        projected = dot(jnp.concatenate([a for _, a in held], axis=0), w_ref[...]).astype(bf16)
+        for at, (r, _) in enumerate(held):
+            rows = pl.ds(pl.multiple_of(r * nodes, nodes), nodes)
+            part[rows, :] = projected[at * nodes : (at + 1) * nodes]
+        held.clear()
         if number == 1:
             for way in (0, 1):
-                start(scatter(0, way))
-        if number == 2:
-            start(scatter(1, near))
-        if number == 4:
-            start(scatter(1, 1 - near))
+                scatter(0, way).start()
 
     absorb([ring + 4], order, finish)
 
+    for way in (0, 1):
+        scatter(0, way).wait_send()
+        start(scatter(1, way))
     for way in (0, 1):
         scatter(0, way).wait_recv()
         rows = block(lax.rem(tp + 1 + 2 * way, 4), way)

time: 62.2 us -> 61.8 us (level)
  no operation moved by 1% of the time
where the time goes in v3:
time: 61.8 us; the launch traced here: 61.6 us
  Pallas kernels  57.8 us (94%)
  local copies, waits for them, and re-layouts  3.11 us (5%)
  between operations  0.64 us (1%)
    pallas_call x1, Pallas kernels, local(): pl.pallas_call(kernel, out_shape=(jax.ShapeDtypeStruct((rows_out, model),...  57.8 us
    unnamed x2, local copies, waits for them, and re-layouts  3.11 us

profile of v3, /device:TPU:1, one launch (start us, length us, event | category | flops | bytes accessed | tf_op | source)
XLA Modules:
  0.0 61.6 jit_solution(12863133573483569004)
XLA Ops:
  0.6 57.8 %verify_attention.1 = (bf16[96,2048]{1,0:T(8,128)(2,1)}, bf16[6,8,256]{2,1,0:T(8,128)(2,1)}) custom-call(s32[6]{0:T(128)} %len_hbm.1, s32[6]{0:T(128)} %group_hbm.1, s32[6,64]{1,0:T(8,128)} %parents_hbm.1, s32[6,8]{1,0:T(8,128)} %accepted_hbm.1, bf16[384,512]{1,0:T(8,128)(2,1)} %q_hbm.1, bf16[384,256]{1,0:T(8,128)(2,1)} %tree_hbm.1, ...), custom_call_target="tpu_custom_call" | custom-call | tf_op jit(solution)/shard_map/verify_attention/pallas_call | solution.py:359
  58.5 1.8 %copy.13 = bf16[96,2048]{1,0:T(8,128)(2,1)} copy(bf16[96,2048]{1,0:T(8,128)(2,1)} %get-tuple-element.4) | data formatting | bytes 786432
  60.2 1.3 %copy.14 = bf16[6,8,256]{2,1,0:T(8,128)(2,1)} copy(bf16[6,8,256]{2,1,0:T(8,128)(2,1)} %get-tuple-element.5) | data formatting | bytes 49152

commit v4 on v3

--- a/solution.py
+++ b/solution.py
@@ -208,16 +208,21 @@
             total = total + dot(vt_ref[block, g], weights)
         return top, total
 
-    def absorb(pieces, order=tuple(range(requests)), done=None):
+    def turn(pieces):
         for block in pieces:
             for g in (0, 1):
                 vt_ref[block, g] = values_t(prompt_refs[block][g, :, hd:])
-        ahead = scores_of(pieces, order[0])
+
+    def absorb(pieces, order=tuple(range(requests)), done=None, fresh=True):
+        if fresh:
+            turn(pieces)
+            pieces = [pieces] * len(order)
+        ahead = scores_of(pieces[0], order[0])
         for number, r in enumerate(order):
             scores = ahead
-            if number + 1 < requests:
-                ahead = scores_of(pieces, order[number + 1])
-            top, total = update(pieces, r, scores)
+            if number + 1 < len(order):
+                ahead = scores_of(pieces[number + 1], order[number + 1])
+            top, total = update(pieces[number], r, scores)
             if done is None:
                 m_ref[r] = top
                 acc_ref[r] = total
@@ -267,8 +272,6 @@
     swapped(3, 5)
     absorb([ring + 3, ring + 5])
     last(1)
-    absorb([4])
-    swapped(4)
     locals_[5].wait()
 
     rows_out = out_ref.shape[0]
@@ -324,7 +327,10 @@
             for way in (0, 1):
                 scatter(0, way).start()
 
-    absorb([ring + 4], order, finish)
+    absorb([4], order[:2])
+    swapped(4)
+    turn([ring + 4])
+    absorb([[ring + 4]] * 2 + [[4, ring + 4]] * (requests - 2), order, finish, False)
 
     for way in (0, 1):
         scatter(0, way).wait_send()

time: 61.8 us -> 62.9 us (1.018)
  Pallas kernels: 57.8 us -> 58.9 us
    pallas_call x1, Pallas kernels: 57.8 us -> 58.9 us  [local(): pl.pallas_call(kernel, out_shape=(jax.ShapeDtypeStruct((rows_out, model),...]
where the time goes in v4:
time: 62.9 us; the launch traced here: 62.7 us
  Pallas kernels  58.9 us (94%)
  local copies, waits for them, and re-layouts  3.11 us (5%)
  between operations  0.64 us (1%)
    pallas_call x1, Pallas kernels, local(): pl.pallas_call(kernel, out_shape=(jax.ShapeDtypeStruct((rows_out, model),...  58.9 us
    unnamed x2, local copies, waits for them, and re-layouts  3.11 us

profile of v4, /device:TPU:1, one launch (start us, length us, event | category | flops | bytes accessed | tf_op | source)
XLA Modules:
  0.0 62.7 jit_solution(7241707384588296556)
XLA Ops:
  0.6 58.9 %verify_attention.1 = (bf16[96,2048]{1,0:T(8,128)(2,1)}, bf16[6,8,256]{2,1,0:T(8,128)(2,1)}) custom-call(s32[6]{0:T(128)} %len_hbm.1, s32[6]{0:T(128)} %group_hbm.1, s32[6,64]{1,0:T(8,128)} %parents_hbm.1, s32[6,8]{1,0:T(8,128)} %accepted_hbm.1, bf16[384,512]{1,0:T(8,128)(2,1)} %q_hbm.1, bf16[384,256]{1,0:T(8,128)(2,1)} %tree_hbm.1, ...), custom_call_target="tpu_custom_call" | custom-call | tf_op jit(solution)/shard_map/verify_attention/pallas_call | solution.py:365
  59.6 1.8 %copy.13 = bf16[96,2048]{1,0:T(8,128)(2,1)} copy(bf16[96,2048]{1,0:T(8,128)(2,1)} %get-tuple-element.4) | data formatting | bytes 786432
  61.3 1.3 %copy.14 = bf16[6,8,256]{2,1,0:T(8,128)(2,1)} copy(bf16[6,8,256]{2,1,0:T(8,128)(2,1)} %get-tuple-element.5) | data formatting | bytes 49152
